TPU v7x, 32 devices: a whole 2x2x4 slice. The times are simulated.
32 devices in a mesh: wide: 8 (over z, x), narrow: 4 (over y, core).
Axes of the slice: x: 2, y: 2, z: 4, core: 2. Of those that a mesh axis runs over, the one named last changes fastest.
Arguments:
- tokens: bfloat16 [16, 1024, 768], P('wide', 'narrow'), may hold values from -6 to 6
- segment_ids: int32 [16, 1024], P('wide'), may hold values from -1 to 7, as said below
- cotangent: bfloat16 [16, 1024, 768], P('wide', 'narrow'), may hold values from -6 to 6
- attn_w: float32 [4, 768, 768], P(None, 'wide', 'narrow')
- attn_m: float32 [4, 768, 768], P(None, 'wide', 'narrow')
- attn_v: float32 [4, 768, 768], P(None, 'wide', 'narrow')
- mlp_w: float32 [2, 768, 3072], P(None, 'wide', 'narrow')
- mlp_m: float32 [2, 768, 3072], P(None, 'wide', 'narrow')
- mlp_v: float32 [2, 768, 3072], P(None, 'wide', 'narrow')
- vectors: float32 [12, 768], replicated
- vec_m: float32 [12, 768], replicated
- vec_v: float32 [12, 768], replicated
Outputs:
- block_out: bfloat16 [16, 1024, 768], P('wide', 'narrow')
- block_input_gradient: float32 [16, 1024, 768], P('wide', 'narrow')
- attn_grad: float32 [4, 768, 768], P(None, 'wide', 'narrow')
- attn_new: float32 [4, 768, 768], P(None, 'wide', 'narrow')
- attn_m_new: float32 [4, 768, 768], P(None, 'wide', 'narrow')
- attn_v_new: float32 [4, 768, 768], P(None, 'wide', 'narrow')
- mlp_grad: float32 [2, 768, 3072], P(None, 'wide', 'narrow')
- mlp_new: float32 [2, 768, 3072], P(None, 'wide', 'narrow')
- mlp_m_new: float32 [2, 768, 3072], P(None, 'wide', 'narrow')
- mlp_v_new: float32 [2, 768, 3072], P(None, 'wide', 'narrow')
- vec_grad: float32 [12, 768], replicated
- vec_new: float32 [12, 768], replicated
- vec_m_new: float32 [12, 768], replicated
- vec_v_new: float32 [12, 768], replicated
Inputs may be any that keep to these rules, and one draw needn't show every extreme that they name: `segment_ids`: in each row the ids start at 0, never fall along the slots and are at most 7; the last slots of a row (at most 51) hold -1 for padding.
All inputs are finite; a program needn't handle non-finite values.
Results may differ from a plain program's by a relative error of at most 0.019.
Values may be sent and summed in bfloat16 or wider, within the bound.
No kernel may reach another device: no remote copies, remote signals or barrier semaphores. Data moves between devices by JAX's collectives and lax.ppermute only.
A program may use at most 128 MiB of HBM per device.

v0:
```python
import jax
import jax.numpy as jnp
from jax import lax
from jax.sharding import PartitionSpec as P

HEAD_DIM = 64
STEP = 10
EPS_NORM = 1e-06
MASKED_SCORE = -1e30
BETA_ONE = 0.5
BETA_TWO = 0.5
EPS_ADAM = 1e-08
RATE_MATRIX = 0.04
RATE_VECTOR = 0.3
DECAY_MATRIX = 0.05


def norm_shard_pieces(values_in, gain_vec, shift_vec):
    row_mean = jnp.mean(values_in, axis=-1, keepdims=True)
    centred = values_in - row_mean
    row_var = jnp.mean(centred * centred, axis=-1, keepdims=True)
    inv_std = lax.rsqrt(row_var + EPS_NORM)
    normed = centred * inv_std
    return (normed * gain_vec + shift_vec, normed, inv_std)


def norm_backward_pass(grad_out, normed, inv_std, gain_vec):
    scaled = grad_out * gain_vec
    return inv_std * (
        scaled
        - jnp.mean(scaled, axis=-1, keepdims=True)
        - normed * jnp.mean(scaled * normed, axis=-1, keepdims=True)
    )


def exact_gelu(values_in):
    return jax.nn.gelu(values_in, approximate=False)


def local_shard_portion(rows_in, sequence_count, start, count):
    shaped = rows_in.reshape(sequence_count, -1, rows_in.shape[-1])
    return lax.dynamic_slice_in_dim(shaped, start, count, 1)


def adamw_update(weight, first_mom, second, gradient, step_rate, decay_rate):
    first_new = BETA_ONE * first_mom + (1.0 - BETA_ONE) * gradient
    second_new = BETA_TWO * second + (1.0 - BETA_TWO) * gradient * gradient
    corrected = (
        first_new
        / (1.0 - BETA_ONE**STEP)
        / (jnp.sqrt(second_new / (1.0 - BETA_TWO**STEP)) + EPS_ADAM)
    )
    return (weight - step_rate * (corrected + decay_rate * weight), first_new, second_new)


def local(
    tokens,
    segment_ids,
    cotangent,
    attn_w,
    attn_m,
    attn_v,
    mlp_w,
    mlp_m,
    mlp_v,
    vectors,
    vec_m,
    vec_v,
):
    narrow_count = lax.axis_size("narrow")
    narrow_index = lax.axis_index("narrow")
    sequence_count, shard_length, width = tokens.shape
    seq_len = segment_ids.shape[1]
    token_count = sequence_count * seq_len
    local_cols = attn_w.shape[2]
    local_hidden = mlp_w.shape[2]
    head_local = local_cols // HEAD_DIM
    block_len = min(seq_len, 512)
    block_count = seq_len // block_len
    scale = HEAD_DIM ** (-0.5)
    shard_offset = narrow_index * shard_length
    attn_full, mlp_full = (
        lax.all_gather(attn_w.astype(jnp.bfloat16), "wide", axis=1, tiled=True),
        lax.all_gather(mlp_w.astype(jnp.bfloat16), "wide", axis=1, tiled=True),
    )
    tokens_all, cot_all = (
        lax.all_gather(tokens, "narrow", axis=1, tiled=True),
        lax.all_gather(cotangent, "narrow", axis=1, tiled=True),
    )
    input_tokens = tokens_all.reshape(token_count, width).astype(jnp.float32)
    cotangent_token_rows = cot_all.reshape(token_count, width)
    own_inputs = tokens.astype(jnp.float32)
    own_cot = cotangent.astype(jnp.float32)
    first_norm_gain = vectors[0]
    first_norm_bias = vectors[1]
    second_norm_gain = vectors[2]
    second_norm_bias = vectors[3]
    out_bias = vectors[4]
    down_bias = vectors[5]
    query_bias = lax.dynamic_slice_in_dim(vectors[6], narrow_index * local_cols, local_cols)
    value_bias = lax.dynamic_slice_in_dim(vectors[7], narrow_index * local_cols, local_cols)
    up_bias = lax.dynamic_slice_in_dim(
        vectors[8:].reshape(-1), narrow_index * local_hidden, local_hidden
    )
    normalized_input, first_standardized, first_inverse_std = norm_shard_pieces(
        input_tokens, first_norm_gain, first_norm_bias
    )
    norm_low = normalized_input.astype(jnp.bfloat16)
    projected = jnp.einsum(
        "td,cde->cte", norm_low, attn_full[:3], preferred_element_type=jnp.float32
    )
    col_bias = jnp.stack([query_bias, jnp.zeros_like(query_bias), value_bias])
    qkv_low = (projected + col_bias[:, None, :]).astype(jnp.bfloat16)
    queries = qkv_low[0].reshape(sequence_count, seq_len, head_local, HEAD_DIM)
    key_rows = qkv_low[1].reshape(sequence_count, seq_len, head_local, HEAD_DIM)
    value_rows = qkv_low[2].reshape(sequence_count, seq_len, head_local, HEAD_DIM)

    def scores_for(block_index):
        row_index = block_index // block_count
        start = block_index % block_count * block_len
        query_block = lax.dynamic_slice_in_dim(
            lax.dynamic_index_in_dim(queries, row_index, 0, False), start, block_len, 0
        )
        key_block = lax.dynamic_index_in_dim(key_rows, row_index, 0, False)
        value_block = lax.dynamic_index_in_dim(value_rows, row_index, 0, False)
        seg_row = lax.dynamic_index_in_dim(segment_ids, row_index, 0, False)
        seg_query = lax.dynamic_slice_in_dim(seg_row, start, block_len, 0)
        raw = (
            jnp.einsum("qhd,khd->hqk", query_block, key_block, preferred_element_type=jnp.float32)
            * scale
        )
        same_doc = seg_query[:, None] == seg_row[None, :]
        masked = jnp.where(same_doc[None], raw, MASKED_SCORE)
        return (masked, query_block, key_block, value_block, row_index, start)

    def attend(block_index):
        masked, query_block, key_block, value_block, row_index, start = scores_for(block_index)
        top_score = jnp.max(masked, axis=-1, keepdims=True)
        expo = jnp.exp(masked - top_score)
        total = jnp.sum(expo, axis=-1, keepdims=True)
        probs_low = (expo / total).astype(jnp.bfloat16)
        context = jnp.einsum(
            "hqk,khd->qhd", probs_low, value_block, preferred_element_type=jnp.float32
        ).astype(jnp.bfloat16)
        return (context, top_score[..., 0] + jnp.log(total[..., 0]))

    block_ids = jnp.arange(sequence_count * block_count)
    contexts, log_totals = lax.map(attend, block_ids)
    context_rows = contexts.reshape(token_count, local_cols)
    out_part = jnp.einsum(
        "tc,dc->td", context_rows, attn_full[3], preferred_element_type=jnp.float32
    )
    out_share = lax.psum_scatter(
        out_part.reshape(sequence_count, seq_len, width), "narrow", scatter_dimension=1, tiled=True
    )
    hidden_own = own_inputs + out_share + out_bias
    normed_two_own, second_standardized_local, inv_two_own = norm_shard_pieces(
        hidden_own, second_norm_gain, second_norm_bias
    )
    second_in = lax.all_gather(
        normed_two_own.astype(jnp.bfloat16), "narrow", axis=1, tiled=True
    ).reshape(token_count, width)
    pre_act = jnp.dot(second_in, mlp_full[0], preferred_element_type=jnp.float32) + up_bias
    activated = exact_gelu(pre_act).astype(jnp.bfloat16)
    down_part = jnp.einsum("tf,df->td", activated, mlp_full[1], preferred_element_type=jnp.float32)
    down_share = lax.psum_scatter(
        down_part.reshape(sequence_count, seq_len, width).astype(jnp.bfloat16),
        "narrow",
        scatter_dimension=1,
        tiled=True,
    ).astype(jnp.float32)
    block_own = hidden_own + down_share + down_bias
    block_out = block_own.astype(jnp.bfloat16)
    grad_down_w = jnp.einsum(
        "td,tf->df", cotangent_token_rows, activated, preferred_element_type=jnp.float32
    )
    grad_act = jnp.dot(cotangent_token_rows, mlp_full[1], preferred_element_type=jnp.float32)
    unused_value, gelu_pull = jax.vjp(exact_gelu, pre_act)
    grad_pre = gelu_pull(grad_act)[0].astype(jnp.bfloat16)
    grad_up_w = jnp.einsum("td,tf->df", second_in, grad_pre, preferred_element_type=jnp.float32)
    grad_up_bias = jnp.sum(grad_pre, axis=0, dtype=jnp.float32)
    norm_two_part = jnp.einsum(
        "tf,df->td", grad_pre, mlp_full[0], preferred_element_type=jnp.float32
    )
    second_norm_local = lax.psum_scatter(
        norm_two_part.reshape(sequence_count, seq_len, width),
        "narrow",
        scatter_dimension=1,
        tiled=True,
    )
    residual_local = own_cot + norm_backward_pass(
        second_norm_local, second_standardized_local, inv_two_own, second_norm_gain
    )
    resid_low = lax.all_gather(
        residual_local.astype(jnp.bfloat16), "narrow", axis=1, tiled=True
    ).reshape(token_count, width)
    grad_out_w = jnp.einsum(
        "td,tc->dc", resid_low, context_rows, preferred_element_type=jnp.float32
    )
    grad_context = jnp.dot(resid_low, attn_full[3], preferred_element_type=jnp.float32).astype(
        jnp.bfloat16
    )
    grad_context = grad_context.reshape(sequence_count, seq_len, head_local, HEAD_DIM)

    def attend_back(block_index):
        masked, query_block, key_block, value_block, row_index, start = scores_for(block_index)
        grad_block = lax.dynamic_slice_in_dim(
            lax.dynamic_index_in_dim(grad_context, row_index, 0, False), start, block_len, 0
        )
        log_block = lax.dynamic_index_in_dim(log_totals, block_index, 0, False)
        probs = jnp.exp(masked - log_block[..., None])
        probs_low = probs.astype(jnp.bfloat16)
        grad_values = jnp.einsum(
            "hqk,qhd->khd", probs_low, grad_block, preferred_element_type=jnp.float32
        )
        grad_probs = jnp.einsum(
            "qhd,khd->hqk", grad_block, value_block, preferred_element_type=jnp.float32
        )
        inner = jnp.sum(probs * grad_probs, axis=-1, keepdims=True)
        grad_scores = (probs * (grad_probs - inner)).astype(jnp.bfloat16)
        grad_query = (
            jnp.einsum("hqk,khd->qhd", grad_scores, key_block, preferred_element_type=jnp.float32)
            * scale
        )
        grad_keys = (
            jnp.einsum("hqk,qhd->khd", grad_scores, query_block, preferred_element_type=jnp.float32)
            * scale
        )
        return (grad_query, grad_keys, grad_values)

    query_parts, key_parts, value_parts = lax.map(attend_back, block_ids)
    grad_query_rows = query_parts.reshape(token_count, local_cols)
    grad_key_rows = (
        key_parts.reshape(sequence_count, block_count, seq_len, local_cols)
        .sum(axis=1)
        .reshape(token_count, local_cols)
    )
    grad_value_rows = (
        value_parts.reshape(sequence_count, block_count, seq_len, local_cols)
        .sum(axis=1)
        .reshape(token_count, local_cols)
    )
    grad_qkv = jnp.stack([grad_query_rows, grad_key_rows, grad_value_rows]).astype(jnp.bfloat16)
    grad_qkv_w = jnp.einsum("td,cte->cde", norm_low, grad_qkv, preferred_element_type=jnp.float32)
    grad_query_bias = jnp.sum(grad_qkv[0], axis=0, dtype=jnp.float32)
    grad_value_bias = jnp.sum(grad_qkv[2], axis=0, dtype=jnp.float32)
    norm_one_part = jnp.einsum(
        "cte,cde->td", grad_qkv, attn_full[:3], preferred_element_type=jnp.float32
    )
    first_norm_local = lax.psum_scatter(
        norm_one_part.reshape(sequence_count, seq_len, width).astype(jnp.bfloat16),
        "narrow",
        scatter_dimension=1,
        tiled=True,
    ).astype(jnp.float32)
    first_standardized_local = local_shard_portion(
        first_standardized, sequence_count, shard_offset, shard_length
    )
    first_inverse_std_local = local_shard_portion(
        first_inverse_std, sequence_count, shard_offset, shard_length
    )
    block_input_gradient = residual_local + norm_backward_pass(
        first_norm_local, first_standardized_local, first_inverse_std_local, first_norm_gain
    )
    fixed_rows = jnp.stack(
        [
            jnp.sum(first_norm_local * first_standardized_local, axis=(0, 1)),
            jnp.sum(first_norm_local, axis=(0, 1)),
            jnp.sum(second_norm_local * second_standardized_local, axis=(0, 1)),
            jnp.sum(second_norm_local, axis=(0, 1)),
            jnp.sum(residual_local, axis=(0, 1)),
            jnp.sum(own_cot, axis=(0, 1)),
        ]
    )
    head_rows = lax.dynamic_update_slice_in_dim(
        jnp.zeros((2, width), jnp.float32),
        jnp.stack([grad_query_bias, grad_value_bias]),
        narrow_index * local_cols,
        1,
    )
    up_rows = lax.dynamic_update_slice_in_dim(
        jnp.zeros((local_hidden * narrow_count,), jnp.float32),
        grad_up_bias,
        narrow_index * local_hidden,
        0,
    ).reshape(-1, width)
    vec_local = jnp.concatenate([fixed_rows, head_rows, up_rows], axis=0)
    vec_grad = lax.psum(vec_local, ("wide", "narrow"))
    attn_local = jnp.concatenate([grad_qkv_w, grad_out_w[None]], axis=0)
    mlp_local = jnp.stack([grad_up_w, grad_down_w])
    attn_grad, mlp_grad = (
        lax.psum_scatter(
            attn_local.astype(jnp.bfloat16), "wide", scatter_dimension=1, tiled=True
        ).astype(jnp.float32),
        lax.psum_scatter(
            mlp_local.astype(jnp.bfloat16), "wide", scatter_dimension=1, tiled=True
        ).astype(jnp.float32),
    )
    attn_new, attn_m_new, attn_v_new = adamw_update(
        attn_w, attn_m, attn_v, attn_grad, RATE_MATRIX, DECAY_MATRIX
    )
    mlp_new, mlp_m_new, mlp_v_new = adamw_update(
        mlp_w, mlp_m, mlp_v, mlp_grad, RATE_MATRIX, DECAY_MATRIX
    )
    vec_new, vec_m_new, vec_v_new = adamw_update(vectors, vec_m, vec_v, vec_grad, RATE_VECTOR, 0.0)
    return (
        block_out,
        block_input_gradient,
        attn_grad,
        attn_new,
        attn_m_new,
        attn_v_new,
        mlp_grad,
        mlp_new,
        mlp_m_new,
        mlp_v_new,
        vec_grad,
        vec_new,
        vec_m_new,
        vec_v_new,
    )


def solution(mesh):
    in_specs = (
        P("wide", "narrow", None),
        P("wide", None),
        P("wide", "narrow", None),
        P(None, "wide", "narrow"),
        P(None, "wide", "narrow"),
        P(None, "wide", "narrow"),
        P(None, "wide", "narrow"),
        P(None, "wide", "narrow"),
        P(None, "wide", "narrow"),
        P(),
        P(),
        P(),
    )
    out_specs = (
        P("wide", "narrow", None),
        P("wide", "narrow", None),
        P(None, "wide", "narrow"),
        P(None, "wide", "narrow"),
        P(None, "wide", "narrow"),
        P(None, "wide", "narrow"),
        P(None, "wide", "narrow"),
        P(None, "wide", "narrow"),
        P(None, "wide", "narrow"),
        P(None, "wide", "narrow"),
        P(),
        P(),
        P(),
        P(),
    )
    return jax.shard_map(local, mesh=mesh, in_specs=in_specs, out_specs=out_specs, check_vma=False)
```

profile of v0, /device:TPU:0, one launch (start us, length us, event | category | flops | bytes accessed | tf_op | source)
XLA Modules:
  0.0 722.1 jit_solution(8954707669613405270)
XLA Ops:
  7.2 1.9 copy.103
  11.9 45.8 %all-gather.9.cloned.1.call-done = bf16[4,768,192]{2,0,1:T(4,128)(2,1)} async-done(((bf16[4,96,192]{2,0,1:T(4,128)(2,1)}), bf16[4,768,192]{2,0,1:T(4,128)(2,1)}) %all-gather.9.cloned.1.call-update) | async-done | bytes 1179664 | tf_op jit(solution)/shard_map/all_gather | solution.py:83
  57.7 2.4 slice.74
  61.5 25.1 %all-gather.7.cloned.1.call-done = bf16[2,1024,768]{2,1,0:T(8,128)(2,1)} async-done(((bf16[2,256,768]{2,1,0:T(8,128)(2,1)}), bf16[2,1024,768]{2,1,0:T(8,128)(2,1)}) %all-gather.7.cloned.1.call-update) | async-done | bytes 3145744 | tf_op jit(solution)/shard_map/all_gather | solution.py:87
  86.6 2.5 convert_reduce_fusion.1
  89.5 3.8 convert_subtract_fusion
  95.2 2.0 fusion.114
  100.1 39.2 %while.32 = (s32[]{:T(128)}, bf16[4,512,3,64]{1,3,2,0:T(8,128)(2,1)}, f32[4,3,512]{2,1,0:T(4,128)S(1)}, s32[4]{0:T(128)S(1)}, bf16[2,1024,3,64]{1,3,2,0:T(8,128)...) while((s32[]{:T(128)}, ...), condition=%wide.region_5.6_spmd, body=%wide.region_2.5_spmd.sunk | while | flops 422148640 | bytes 22229476 | solution.py:148
  105.3 1.7 fusion.151
  107.1 2.7 fusion.152
  115.1 1.7 fusion.151
  116.8 2.7 fusion.152
  124.8 1.7 fusion.151
  126.5 2.7 fusion.152
  136.2 2.7 fusion.152
  139.3 2.0 copy.70
  142.8 4.8 fusion.97
  149.5 56.7 %reduce-scatter.9.cloned.1.call-done = f32[2,256,768]{2,1,0:T(8,128)} async-done(((f32[2,1024,768]{2,1,0:T(8,128)}), f32[2,256,768]{2,1,0:T(8,128)}) %reduce-scatter.9.cloned.1.call-update) | async-done | bytes 1572880 | tf_op jit(solution)/shard_map/reduce_scatter | solution.py:153
  206.1 1.9 fusion.111
  210.3 50.6 %all-gather.13.cloned.1.call-done = bf16[2,768,768]{2,1,0:T(8,128)(2,1)} async-done(((bf16[2,96,768]{2,1,0:T(8,128)(2,1)}), bf16[2,768,768]{2,1,0:T(8,128)(2,1)}) %all-gather.13.cloned.1.call-update) | async-done | bytes 2359312 | tf_op jit(solution)/shard_map/all_gather | solution.py:84
  261.0 29.2 %all-gather.11.cloned.1.call-done = bf16[2,1024,768]{2,1,0:T(8,128)(2,1)} async-done(((bf16[2,256,768]{2,1,0:T(8,128)(2,1)}), bf16[2,1024,768]{2,1,0:T(8,128)(2,1)}) %all-gather.11.cloned.1.call-update) | async-done | bytes 3145744 | tf_op jit(solution)/shard_map/all_gather | solution.py:160
  290.1 19.0 %multiply_convert_fusion.1 = (bf16[2048,768]{1,0:T(8,128)(2,1)}, f32[2048,768]{1,0:T(8,128)}, f32[2048,768]{1,0:T(8,128)}) fusion(f32[768]{0:T(1024)S(1)} %dynamic_slice.110, bf16[2048,768]{1,0:T(8,128)(2,1)} %bitcast.256, bf16[2,768,768]{2,1,0:T(8,128)(2,1)} %all-gather.13.cloned.1.call-done), kind=kOutput, calls=%fused_computation.73 | convolution fusion | flops 2519728128 | bytes 20057088 | tf_op jit(solution)/shard_map/dot_general | solution.py:163
  309.1 11.1 %all-gather.15.cloned.1.call-done = bf16[2,1024,768]{2,1,0:T(8,128)(2,1)} async-done(((bf16[2,256,768]{2,1,0:T(8,128)(2,1)}), bf16[2,1024,768]{2,1,0:T(8,128)(2,1)}) %all-gather.15.cloned.1.call-update) | async-done | bytes 3145744 | tf_op jit(solution)/shard_map/all_gather | solution.py:88
  320.2 10.6 %convert_reduce_fusion = (f32[768]{0:T(1024)S(1)}, bf16[2048,768]{1,0:T(8,128)(2,1)S(1)}) fusion(f32[2048,768]{1,0:T(8,128)} %get-tuple-element.504, bf16[2048,768]{1,0:T(8,128)(2,1)} %bitcast.258, bf16[2,768,768]{2,1,0:T(8,128)(2,1)} %all-gather.13.cloned.1.call-done, f32[2048,768]{1,0:T(8,128)} %get-tuple-element.530, f32[768]{0:T(1024)S(1)} %dynamic_slice.110), kind=kOutput, calls=%fused_computation.71 | convolution fusion | flops 2442657024 | bytes 20060160 | tf_op jit(solution)/shard_map/dot_general | solution.py:177
  332.5 4.5 fusion.83
  337.0 6.6 convolution_convert_fusion.1
  343.9 51.6 %reduce-scatter.13.cloned.1.call-done = f32[2,256,768]{2,1,0:T(8,128)} async-done(((f32[2,1024,768]{2,1,0:T(8,128)}), f32[2,256,768]{2,1,0:T(8,128)}) %reduce-scatter.13.cloned.1.call-update) | async-done | bytes 1572880 | tf_op jit(solution)/shard_map/reduce_scatter | solution.py:185
  395.5 2.1 multiply_reduce_fusion.2
  397.6 38.4 %reduce-scatter.11.cloned.1.call-done = bf16[2,256,768]{2,1,0:T(8,128)(2,1)} async-done(((bf16[2,1024,768]{2,1,0:T(8,128)(2,1)}), bf16[2,256,768]{2,1,0:T(8,128)(2,1)}) %reduce-scatter.11.cloned.1.call-update) | async-done | bytes 786448 | tf_op jit(solution)/shard_map/reduce_scatter | solution.py:166
  436.1 3.6 fusion.107
  442.9 5.6 fusion.79
  448.6 2.7 fusion.78
  453.0 17.5 %all-gather.17.cloned.1.call-done = bf16[2,1024,768]{2,1,0:T(8,128)(2,1)} async-done(((bf16[2,256,768]{2,1,0:T(8,128)(2,1)}), bf16[2,1024,768]{2,1,0:T(8,128)(2,1)}) %all-gather.17.cloned.1.call-update) | async-done | bytes 3145744 | tf_op jit(solution)/shard_map/all_gather | solution.py:194
  470.5 3.1 convolution_convert_fusion
  476.4 64.6 %while.33 = (s32[]{:T(128)}, bf16[4,512,3,64]{1,3,2,0:T(8,128)(2,1)}, f32[4,1024,3,64]{1,3,2,0:T(8,128)}, f32[4,1024,3,64]{1,3,2,0:T(8,128)}, s32[4]{0:T(128)S(1...) while((s32[]{:T(128)}, ...), condition=%wide.region_15.16_spmd, body=%wide.region_13.15_spmd.sunk | while | flops 1031043584 | bytes 59572856 | solution.py:231
  482.7 2.8 fusion.164
  485.5 2.6 multiply_reduce_fusion.7
  488.1 1.8 multiply_convert_fusion.3
  498.8 2.8 fusion.164
  501.6 2.6 multiply_reduce_fusion.7
  504.2 1.8 multiply_convert_fusion.3
  514.9 2.8 fusion.164
  517.7 2.6 multiply_reduce_fusion.7
  520.3 1.8 multiply_convert_fusion.3
  530.9 2.8 fusion.164
  533.8 2.6 multiply_reduce_fusion.7
  536.4 1.8 multiply_convert_fusion.3
  541.0 2.3 reduce_sum.204
  543.2 2.3 reduce_sum.203
  548.4 2.6 copy.77
  551.0 2.3 stack_reshape.12
  553.6 2.5 copy-done.11
  557.1 2.0 fusion.80
  560.2 2.6 copy.91
  562.9 2.3 reshape.314
  565.2 6.2 bitcast_convert_fusion
  574.9 2.9 multiply_subtract_fusion
  578.4 50.8 %reduce-scatter.19.cloned.1.call-done = bf16[96,768]{1,0:T(8,128)(2,1)} async-done(((bf16[768,768]{1,0:T(8,128)(2,1)}), bf16[96,768]{1,0:T(8,128)(2,1)}) %reduce-scatter.19.cloned.1.call-update) | async-done | bytes 147472
  632.6 2.1 copy.87
  634.7 1.9 copy.88
  637.5 31.3 %reduce-scatter.15.cloned.1.call-done = bf16[2,256,768]{2,1,0:T(8,128)(2,1)} async-done(((bf16[2,1024,768]{2,1,0:T(8,128)(2,1)}), bf16[2,256,768]{2,1,0:T(8,128)(2,1)}) %reduce-scatter.15.cloned.1.call-update) | async-done | bytes 786448 | tf_op jit(solution)/shard_map/reduce_scatter | solution.py:250
  668.8 2.4 fusion.74
  671.3 39.7 %psum.7 = f32[12,768]{1,0:T(8,128)S(1)} all-reduce(f32[12,768]{1,0:T(8,128)S(1)} %concatenate.8), channel_id=1, replica_groups=mesh['wide'=8,'narrow'=4] {'wide','narrow'}, use_global_device_ids=true, to_apply=%region_32.33 | all-reduce | flops 9216 | bytes 73728 | tf_op jit(solution)/shard_map/psum | solution.py:288
  711.8 3.0 fusion.72
  (237 shorter events, 70.3 us)
Async XLA Ops:
  7.2 50.5 %all-gather.9.cloned.1.call-start = ((), (), s32[]{:S(2)}) async-start(), calls=%async_computation.7 | async-start | bytes 1769472 | tf_op jit(solution)/shard_map/all_gather | solution.py:83
  9.2 77.4 %all-gather.7.cloned.1.call-start = ((), (), s32[]{:S(2)}) async-start(), calls=%async_computation.6 | async-start | bytes 3932160 | tf_op jit(solution)/shard_map/all_gather | solution.py:87
  9.9 196.2 %reduce-scatter.9.cloned.1.call-start = ((), (), s32[]{:S(2)}) async-start(), calls=%async_computation.8 | async-start | bytes 7864320 | tf_op jit(solution)/shard_map/reduce_scatter | solution.py:153
  11.8 82.1 %copy-start.24 = (f32[768]{0:T(1024)}, f32[768]{0:T(1024)S(1)}, u32[]{:S(2)}) copy-start(f32[768]{0:T(1024)S(1)} %get-tuple-element.520) | copy-start | bytes 9220
  57.7 2.9 copy-start.7
  61.5 33.7 %copy-start.16 = (bf16[3,768,192]{1,2,0:T(8,128)(2,1)}, bf16[3,768,192]{1,2,0:T(8,128)(2,1)S(1)}, u32[]{:S(2)}) copy-start(bf16[3,768,192]{1,2,0:T(8,128)(2,1)S(1)} %copy.93) | copy-start | bytes 2654212
  86.6 2.8 copy-start
  95.1 2.1 copy-start.9
  98.5 1.6 copy-start.19
  139.3 8.3 %copy-start.3 = (bf16[2,1024,3,64]{1,3,2,0:T(8,128)(2,1)}, bf16[2,1024,3,64]{1,3,2,0:T(8,128)(2,1)S(1)}, u32[]{:S(2)}) copy-start(bf16[2,1024,3,64]{1,3,2,0:T(8,128)(2,1)S(1)} %get-tuple-element.774) | copy-start | bytes 2359300
  141.4 6.2 copy-start.5
  147.6 1.1 copy-start.13
  147.6 113.3 %all-gather.13.cloned.1.call-start = ((), (), s32[]{:S(2)}) async-start(), calls=%async_computation.10 | async-start | bytes 2654208 | tf_op jit(solution)/shard_map/all_gather | solution.py:84
  149.4 140.7 %all-gather.11.cloned.1.call-start = ((), (), s32[]{:S(2)}) async-start(), calls=%async_computation.9 | async-start | bytes 3932160 | tf_op jit(solution)/shard_map/all_gather | solution.py:160
  208.0 2.2 slice-start
  209.6 110.6 %all-gather.15.cloned.1.call-start = ((), (), s32[]{:S(2)}) async-start(), calls=%async_computation.12 | async-start | bytes 3932160 | tf_op jit(solution)/shard_map/all_gather | solution.py:88
  210.2 185.3 %reduce-scatter.13.cloned.1.call-start = ((), (), s32[]{:S(2)}) async-start(), calls=%async_computation.13 | async-start | bytes 7864320 | tf_op jit(solution)/shard_map/reduce_scatter | solution.py:185
  320.2 12.3 %copy-start.30 = (bf16[2,768,768]{2,1,0:T(8,128)(2,1)S(1)}, bf16[2,768,768]{2,1,0:T(8,128)(2,1)}, u32[]{:S(2)}) copy-start(bf16[2,768,768]{2,1,0:T(8,128)(2,1)} %all-gather.13.cloned.1.call-done) | copy-start | bytes 7077892
  330.8 1.7 copy-start.31
  337.0 99.1 %reduce-scatter.11.cloned.1.call-start = ((), (), s32[]{:S(2)}) async-start(), calls=%async_computation.11 | async-start | bytes 3932160 | tf_op jit(solution)/shard_map/reduce_scatter | solution.py:166
  343.6 92.4 %copy-start.28 = (f32[768]{0:T(1024)S(1)}, f32[768]{0:T(1024)}, u32[]{:S(2)}) copy-start(f32[768]{0:T(1024)} %get-tuple-element.525) | copy-start | bytes 9220
  343.7 126.8 %all-gather.17.cloned.1.call-start = ((), (), s32[]{:S(2)}) async-start(), calls=%async_computation.14 | async-start | bytes 3932160 | tf_op jit(solution)/shard_map/all_gather | solution.py:194
  439.6 1.1 copy-start.1
  439.6 2.2 copy-start.6
  441.8 133.1 %reduce-scatter.17.cloned.1.call-start = ((), (), s32[]{:S(2)}) async-start(), calls=%async_computation.16 | async-start | bytes 2654208 | tf_op jit(solution)/shard_map/reduce_scatter | solution.py:295
  442.9 5.7 copy-start.29
  442.9 5.7 copy-start.32
  452.9 176.3 %reduce-scatter.19.cloned.1.call-start = ((), (), s32[]{:S(2)}) async-start(), calls=%async_computation.17 | async-start | bytes 1327104
  473.5 2.8 copy-start.4
  488.1 1.8 copy-start.17
  491.0 1.6 copy-start.18
  504.2 1.8 copy-start.17
  507.1 1.7 copy-start.18
  520.3 1.8 copy-start.17
  523.2 1.6 copy-start.18
  536.4 1.8 copy-start.17
  539.3 1.6 copy-start.18
  551.0 2.6 copy-start.8
  553.4 2.7 copy-start.11
  553.5 3.6 copy-start.10
  553.6 5.5 copy-start.21
  565.1 103.7 %reduce-scatter.15.cloned.1.call-start = ((), (), s32[]{:S(2)}) async-start(), calls=%async_computation.15 | async-start | bytes 3932160 | tf_op jit(solution)/shard_map/reduce_scatter | solution.py:250
  571.4 1.0 copy-start.15
  571.4 1.2 copy-start.20
  571.4 3.5 copy-start.14
  578.2 90.6 %copy-start.25 = (f32[768]{0:T(1024)S(1)}, f32[768]{0:T(1024)}, u32[]{:S(2)}) copy-start(f32[768]{0:T(1024)} %copy-done.24) | copy-start | bytes 9220
  631.4 79.6 %copy-start.23 = (f32[12,768]{1,0:T(8,128)S(1)}, f32[12,768]{1,0:T(8,128)}, u32[]{:S(2)}) copy-start(f32[12,768]{1,0:T(8,128)} %param.25) | copy-start | bytes 110596
  631.4 79.6 %copy-start.26 = (f32[12,768]{1,0:T(8,128)S(1)}, f32[12,768]{1,0:T(8,128)}, u32[]{:S(2)}) copy-start(f32[12,768]{1,0:T(8,128)} %param.26) | copy-start | bytes 110596
  631.4 79.6 %copy-start.27 = (f32[12,768]{1,0:T(8,128)S(1)}, f32[12,768]{1,0:T(8,128)}, u32[]{:S(2)}) copy-start(f32[12,768]{1,0:T(8,128)} %param.27) | copy-start | bytes 110596
  632.6 79.2 %copy-start.2 = (f32[2,256,768]{2,1,0:T(8,128)S(1)}, f32[2,256,768]{2,1,0:T(8,128)}, u32[]{:S(2)}) copy-start(f32[2,256,768]{2,1,0:T(8,128)} %copy-done.1) | copy-start | bytes 4718596
  668.8 43.0 %copy-start.12 = (bf16[2,256,768]{2,1,0:T(8,128)(2,1)S(1)}, bf16[2,256,768]{2,1,0:T(8,128)(2,1)}, u32[]{:S(2)}) copy-start(bf16[2,256,768]{2,1,0:T(8,128)(2,1)} %reduce-scatter.15.cloned.1.call-done) | copy-start | bytes 2359300
  711.1 3.7 copy-start.22
Sparse Core Ops, SparseCore 0:
  10.8 46.8 all-gather.8
  59.2 27.3 all-gather.6
  147.8 58.3 reduce-scatter.8
  209.0 51.9 all-gather.12
  263.0 27.0 all-gather.10
  291.6 28.5 all-gather.14
  337.1 58.3 reduce-scatter.12
  398.0 37.9 reduce-scatter.10
  441.9 28.5 all-gather.16
  474.2 69.1 reduce-scatter.16
  565.3 63.9 reduce-scatter.18
  631.8 36.9 reduce-scatter.14
where the time goes:
time: 732 us; the launch traced here: 722 us
  waiting for transfers between devices  409 us (56%)
  matrix products  122 us (17%)
  other arithmetic  54.4 us (7%)
  local copies, waits for them, and re-layouts  53.4 us (7%)
  blocking collectives  39.7 us (5%)
  loops' own time  27.1 us (4%)
  between operations  15.4 us (2%)
    reduce_scatter x1, waiting for transfers between devices, local(): lax.psum_scatter(out_part.reshape(sequence_count, seq_len, width), 'narro...  56.7 us
    unnamed x13, waiting for transfers between devices  52.2 us
    reduce_scatter x1, waiting for transfers between devices, local(): lax.psum_scatter(norm_two_part.reshape(sequence_count, seq_len, width), '...  51.6 us
    all_gather x1, waiting for transfers between devices, local(): lax.all_gather(mlp_w.astype(jnp.bfloat16), 'wide', axis=1, tiled=True)  50.6 us
    all_gather x1, waiting for transfers between devices, local(): lax.all_gather(attn_w.astype(jnp.bfloat16), 'wide', axis=1, tiled=True)  45.8 us
    psum x1, blocking collectives, local(): vec_grad = lax.psum(vec_local, ('wide', 'narrow'))  39.7 us
    reduce_scatter x1, waiting for transfers between devices, local(): lax.psum_scatter(down_part.reshape(sequence_count, seq_len, width).astype...  38.4 us
    reduce_scatter x1, waiting for transfers between devices, local(): lax.psum_scatter(norm_one_part.reshape(sequence_count, seq_len, width).as...  31.3 us
  transfers between devices with their start and end apart: 12, of which 11 were waited for; matrix products, arithmetic and copies ran while one was open for 20% of the time, Pallas kernels for 0%

commit v1 on v0

--- a/solution.py
+++ b/solution.py
@@ -13,6 +13,18 @@
 RATE_MATRIX = 0.04
 RATE_VECTOR = 0.3
 DECAY_MATRIX = 0.05
+
+
+def doubled_up(x, axis, dim):
+    ways, here, lap = (lax.axis_size(axis), lax.axis_index(axis), x.shape[dim])
+    line, have = (x, 1)
+    while have < ways:
+        line = jnp.concatenate(
+            [line, lax.ppermute(line, axis, [(d, (d - have) % ways) for d in range(ways)])],
+            axis=dim,
+        )
+        have = 2 * have
+    return jnp.roll(line, here * lap, axis=dim)
 
 
 def norm_shard_pieces(values_in, gain_vec, shift_vec):
@@ -191,9 +203,9 @@
     residual_local = own_cot + norm_backward_pass(
         second_norm_local, second_standardized_local, inv_two_own, second_norm_gain
     )
-    resid_low = lax.all_gather(
-        residual_local.astype(jnp.bfloat16), "narrow", axis=1, tiled=True
-    ).reshape(token_count, width)
+    resid_low = doubled_up(residual_local.astype(jnp.bfloat16), "narrow", 1).reshape(
+        token_count, width
+    )
     grad_out_w = jnp.einsum(
         "td,tc->dc", resid_low, context_rows, preferred_element_type=jnp.float32
     )

time: 732 us -> 764 us (1.044)
  waiting for transfers between devices: 409 us -> 427 us
  local copies, waits for them, and re-layouts: 53.4 us -> 66.5 us
    ppermute x0 -> x2, waiting for transfers between devices: none -> 33.9 us  [doubled_up(): lax.ppermute(line, axis, [(d, (d - have) % ways) for d in range(ways)])]
    all_gather x1 -> x0, waiting for transfers between devices: 17.5 us -> none  [local(): lax.all_gather(residual_local.astype(jnp.bfloat16), 'narrow', axis=1, til...]
    unnamed x79 -> x87, local copies, waits for them, and re-layouts: 25.9 us -> 34.2 us
    unnamed x13 -> x12, waiting for transfers between devices: 52.2 us -> 53.7 us
  transfers between devices with their start and end apart: 12 -> 13, of which waited for: 11 -> 12; matrix products, arithmetic and copies ran while one was open for 20% -> 20% of each run, Pallas kernels for 0% -> 0%
where the time goes in v1:
time: 764 us; the launch traced here: 754 us
  waiting for transfers between devices  427 us (56%)
  matrix products  119 us (16%)
  local copies, waits for them, and re-layouts  66.5 us (9%)
  other arithmetic  57.1 us (7%)
  blocking collectives  39.7 us (5%)
  loops' own time  27.1 us (4%)
  between operations  15 us (2%)
    reduce_scatter x1, waiting for transfers between devices, local(): lax.psum_scatter(out_part.reshape(sequence_count, seq_len, width), 'narro...  56.7 us
    unnamed x12, waiting for transfers between devices  53.7 us
    reduce_scatter x1, waiting for transfers between devices, local(): lax.psum_scatter(norm_two_part.reshape(sequence_count, seq_len, width), '...  51.6 us
    all_gather x1, waiting for transfers between devices, local(): lax.all_gather(mlp_w.astype(jnp.bfloat16), 'wide', axis=1, tiled=True)  50.6 us
    all_gather x1, waiting for transfers between devices, local(): lax.all_gather(attn_w.astype(jnp.bfloat16), 'wide', axis=1, tiled=True)  45.8 us
    psum x1, blocking collectives, local(): vec_grad = lax.psum(vec_local, ('wide', 'narrow'))  39.7 us
    reduce_scatter x1, waiting for transfers between devices, local(): lax.psum_scatter(down_part.reshape(sequence_count, seq_len, width).astype...  38.4 us
    unnamed x87, local copies, waits for them, and re-layouts  34.2 us
  transfers between devices with their start and end apart: 13, of which 12 were waited for; matrix products, arithmetic and copies ran while one was open for 20% of the time, Pallas kernels for 0%

profile of v1, /device:TPU:0, one launch (start us, length us, event | category | flops | bytes accessed | tf_op | source)
XLA Modules:
  0.0 754.3 jit_solution(10677976137465858124)
XLA Ops:
  7.2 1.9 copy.103
  11.9 45.8 %all-gather.8.cloned.1.call-done = bf16[4,768,192]{2,0,1:T(4,128)(2,1)} async-done(((bf16[4,96,192]{2,0,1:T(4,128)(2,1)}), bf16[4,768,192]{2,0,1:T(4,128)(2,1)}) %all-gather.8.cloned.1.call-update) | async-done | bytes 1179664 | tf_op jit(solution)/shard_map/all_gather | solution.py:95
  57.7 2.4 slice.74
  61.5 25.1 %all-gather.6.cloned.1.call-done = bf16[2,1024,768]{2,1,0:T(8,128)(2,1)} async-done(((bf16[2,256,768]{2,1,0:T(8,128)(2,1)}), bf16[2,1024,768]{2,1,0:T(8,128)(2,1)}) %all-gather.6.cloned.1.call-update) | async-done | bytes 3145744 | tf_op jit(solution)/shard_map/all_gather | solution.py:99
  86.6 2.5 convert_reduce_fusion.1
  89.5 3.8 convert_subtract_fusion
  95.2 2.0 fusion.114
  100.1 39.2 %while.32 = (s32[]{:T(128)}, bf16[4,512,3,64]{1,3,2,0:T(8,128)(2,1)}, f32[4,3,512]{2,1,0:T(4,128)S(1)}, s32[4]{0:T(128)S(1)}, bf16[2,1024,3,64]{1,3,2,0:T(8,128)...) while((s32[]{:T(128)}, ...), condition=%wide.region_5.6_spmd, body=%wide.region_2.5_spmd.sunk | while | flops 422148640 | bytes 22229476 | solution.py:160
  107.1 2.7 fusion.152
  116.8 2.7 fusion.152
  126.5 2.7 fusion.152
  136.2 2.7 fusion.152
  139.3 2.0 copy.70
  142.8 4.8 fusion.97
  149.5 56.7 %reduce-scatter.9.cloned.1.call-done = f32[2,256,768]{2,1,0:T(8,128)} async-done(((f32[2,1024,768]{2,1,0:T(8,128)}), f32[2,256,768]{2,1,0:T(8,128)}) %reduce-scatter.9.cloned.1.call-update) | async-done | bytes 1572880 | tf_op jit(solution)/shard_map/reduce_scatter | solution.py:165
  206.1 1.9 fusion.111
  210.3 50.6 %all-gather.12.cloned.1.call-done = bf16[2,768,768]{2,1,0:T(8,128)(2,1)} async-done(((bf16[2,96,768]{2,1,0:T(8,128)(2,1)}), bf16[2,768,768]{2,1,0:T(8,128)(2,1)}) %all-gather.12.cloned.1.call-update) | async-done | bytes 2359312 | tf_op jit(solution)/shard_map/all_gather | solution.py:96
  261.0 29.2 %all-gather.10.cloned.1.call-done = bf16[2,1024,768]{2,1,0:T(8,128)(2,1)} async-done(((bf16[2,256,768]{2,1,0:T(8,128)(2,1)}), bf16[2,1024,768]{2,1,0:T(8,128)(2,1)}) %all-gather.10.cloned.1.call-update) | async-done | bytes 3145744 | tf_op jit(solution)/shard_map/all_gather | solution.py:172
  290.1 19.0 %multiply_convert_fusion.1 = (bf16[2048,768]{1,0:T(8,128)(2,1)}, f32[2048,768]{1,0:T(8,128)}, f32[2048,768]{1,0:T(8,128)}) fusion(f32[768]{0:T(1024)S(1)} %dynamic_slice.114, bf16[2048,768]{1,0:T(8,128)(2,1)} %bitcast.256, bf16[2,768,768]{2,1,0:T(8,128)(2,1)} %all-gather.12.cloned.1.call-done), kind=kOutput, calls=%fused_computation.73 | convolution fusion | flops 2519728128 | bytes 20057088 | tf_op jit(solution)/shard_map/dot_general | solution.py:175
  309.1 11.1 %all-gather.14.cloned.1.call-done = bf16[2,1024,768]{2,1,0:T(8,128)(2,1)} async-done(((bf16[2,256,768]{2,1,0:T(8,128)(2,1)}), bf16[2,1024,768]{2,1,0:T(8,128)(2,1)}) %all-gather.14.cloned.1.call-update) | async-done | bytes 3145744 | tf_op jit(solution)/shard_map/all_gather | solution.py:100
  320.2 10.6 %convert_reduce_fusion = (f32[768]{0:T(1024)S(1)}, bf16[2048,768]{1,0:T(8,128)(2,1)S(1)}) fusion(f32[2048,768]{1,0:T(8,128)} %get-tuple-element.506, bf16[2048,768]{1,0:T(8,128)(2,1)} %bitcast.258, bf16[2,768,768]{2,1,0:T(8,128)(2,1)} %all-gather.12.cloned.1.call-done, f32[2048,768]{1,0:T(8,128)} %get-tuple-element.532, f32[768]{0:T(1024)S(1)} %dynamic_slice.114), kind=kOutput, calls=%fused_computation.71 | convolution fusion | flops 2442657024 | bytes 20060160 | tf_op jit(solution)/shard_map/dot_general | solution.py:189
  332.5 4.5 fusion.83
  337.0 6.6 convolution_convert_fusion.1
  343.9 51.6 %reduce-scatter.13.cloned.1.call-done = f32[2,256,768]{2,1,0:T(8,128)} async-done(((f32[2,1024,768]{2,1,0:T(8,128)}), f32[2,256,768]{2,1,0:T(8,128)}) %reduce-scatter.13.cloned.1.call-update) | async-done | bytes 1572880 | tf_op jit(solution)/shard_map/reduce_scatter | solution.py:197
  395.5 2.1 multiply_reduce_fusion.2
  397.6 38.4 %reduce-scatter.11.cloned.1.call-done = bf16[2,256,768]{2,1,0:T(8,128)(2,1)} async-done(((bf16[2,1024,768]{2,1,0:T(8,128)(2,1)}), bf16[2,256,768]{2,1,0:T(8,128)(2,1)}) %reduce-scatter.11.cloned.1.call-update) | async-done | bytes 786448 | tf_op jit(solution)/shard_map/reduce_scatter | solution.py:178
  436.0 3.6 fusion.107
  443.1 8.7 %collective-permute-done = bf16[2,256,768]{2,1,0:T(8,128)(2,1)S(1)} collective-permute-done((bf16[2,256,768]{2,1,0:T(8,128)(2,1)}, bf16[2,256,768]{2,1,0:T(8,128)(2,1)S(1)}, u32[]{:S(2)}, u32[]{:S(2)}) %collective-permute-start) | collective-permute-done | bytes 786464 | tf_op jit(solution)/shard_map/ppermute | solution.py:23
  451.8 2.4 pad_maximum_fusion.1
  455.7 4.9 fusion.79
  460.7 2.7 fusion.78
  466.0 25.2 %collective-permute-done.1 = bf16[2,512,768]{2,1,0:T(8,128)(2,1)} collective-permute-done((bf16[2,512,768]{2,1,0:T(8,128)(2,1)}, bf16[2,512,768]{2,1,0:T(8,128)(2,1)}, u32[]{:S(2)}, u32[]{:S(2)}) %collective-permute-start.1) | collective-permute-done | bytes 1572896 | tf_op jit(solution)/shard_map/ppermute | solution.py:23
  491.2 2.7 constant_dynamic-update-slice_fusion.3
  493.9 2.1 constant_dynamic-update-slice_fusion.2
  496.9 2.7 constant_dynamic-update-slice_fusion
  499.6 2.1 constant_dynamic-slice_fusion.2
  507.4 64.5 %while.33 = (s32[]{:T(128)}, bf16[4,512,3,64]{1,3,2,0:T(8,128)(2,1)}, f32[4,1024,3,64]{1,3,2,0:T(8,128)}, f32[4,1024,3,64]{1,3,2,0:T(8,128)}, s32[4]{0:T(128)S(1...) while((s32[]{:T(128)}, ...), condition=%wide.region_15.16_spmd, body=%wide.region_13.15_spmd.sunk | while | flops 1031043584 | bytes 59572856 | solution.py:243
  513.8 2.8 fusion.164
  516.6 2.6 multiply_reduce_fusion.7
  529.9 2.8 fusion.164
  532.7 2.6 multiply_reduce_fusion.7
  535.3 1.8 multiply_convert_fusion.3
  545.9 2.8 fusion.164
  548.7 2.6 multiply_reduce_fusion.7
  551.3 1.8 multiply_convert_fusion.3
  562.0 2.8 fusion.164
  564.8 2.6 multiply_reduce_fusion.7
  572.0 2.3 reduce_sum.204
  574.2 2.3 reduce_sum.203
  579.4 2.6 copy.77
  582.0 2.3 stack_reshape.12
  584.5 2.5 copy-done.4
  588.1 2.0 fusion.80
  591.2 2.6 copy.91
  593.8 2.3 reshape.314
  596.2 6.2 bitcast_convert_fusion
  605.9 2.9 multiply_subtract_fusion
  609.4 52.3 %reduce-scatter.19.cloned.1.call-done = bf16[96,768]{1,0:T(8,128)(2,1)} async-done(((bf16[768,768]{1,0:T(8,128)(2,1)}), bf16[96,768]{1,0:T(8,128)(2,1)}) %reduce-scatter.19.cloned.1.call-update) | async-done | bytes 147472
  665.1 2.1 copy.87
  667.1 1.9 copy.88
  670.0 31.4 %reduce-scatter.15.cloned.1.call-done = bf16[2,256,768]{2,1,0:T(8,128)(2,1)} async-done(((bf16[2,1024,768]{2,1,0:T(8,128)(2,1)}), bf16[2,256,768]{2,1,0:T(8,128)(2,1)}) %reduce-scatter.15.cloned.1.call-update) | async-done | bytes 786448 | tf_op jit(solution)/shard_map/reduce_scatter | solution.py:262
  701.4 2.4 fusion.74
  703.9 39.7 %psum.7 = f32[12,768]{1,0:T(8,128)S(1)} all-reduce(f32[12,768]{1,0:T(8,128)S(1)} %concatenate.20), channel_id=1, replica_groups=mesh['wide'=8,'narrow'=4] {'wide','narrow'}, use_global_device_ids=true, to_apply=%region_32.33 | all-reduce | flops 9216 | bytes 73728 | tf_op jit(solution)/shard_map/psum | solution.py:300
  744.3 3.0 fusion.72
  (249 shorter events, 85.5 us)
Async XLA Ops:
  7.2 50.5 %all-gather.8.cloned.1.call-start = ((), (), s32[]{:S(2)}) async-start(), calls=%async_computation.7 | async-start | bytes 1769472 | tf_op jit(solution)/shard_map/all_gather | solution.py:95
  9.2 77.4 %all-gather.6.cloned.1.call-start = ((), (), s32[]{:S(2)}) async-start(), calls=%async_computation.6 | async-start | bytes 3932160 | tf_op jit(solution)/shard_map/all_gather | solution.py:99
  9.9 196.2 %reduce-scatter.9.cloned.1.call-start = ((), (), s32[]{:S(2)}) async-start(), calls=%async_computation.8 | async-start | bytes 7864320 | tf_op jit(solution)/shard_map/reduce_scatter | solution.py:165
  11.8 82.1 %copy-start.25 = (f32[768]{0:T(1024)}, f32[768]{0:T(1024)S(1)}, u32[]{:S(2)}) copy-start(f32[768]{0:T(1024)S(1)} %get-tuple-element.522) | copy-start | bytes 9220
  57.7 2.9 copy-start.9
  61.5 33.7 %copy-start.17 = (bf16[3,768,192]{1,2,0:T(8,128)(2,1)}, bf16[3,768,192]{1,2,0:T(8,128)(2,1)S(1)}, u32[]{:S(2)}) copy-start(bf16[3,768,192]{1,2,0:T(8,128)(2,1)S(1)} %copy.93) | copy-start | bytes 2654212
  86.6 2.8 copy-start
  95.1 2.1 copy-start.11
  98.5 1.6 copy-start.20
  139.3 8.3 %copy-start.5 = (bf16[2,1024,3,64]{1,3,2,0:T(8,128)(2,1)}, bf16[2,1024,3,64]{1,3,2,0:T(8,128)(2,1)S(1)}, u32[]{:S(2)}) copy-start(bf16[2,1024,3,64]{1,3,2,0:T(8,128)(2,1)S(1)} %get-tuple-element.775) | copy-start | bytes 2359300
  141.4 6.2 copy-start.7
  147.6 1.1 copy-start.14
  147.6 113.3 %all-gather.12.cloned.1.call-start = ((), (), s32[]{:S(2)}) async-start(), calls=%async_computation.10 | async-start | bytes 2654208 | tf_op jit(solution)/shard_map/all_gather | solution.py:96
  149.4 140.7 %all-gather.10.cloned.1.call-start = ((), (), s32[]{:S(2)}) async-start(), calls=%async_computation.9 | async-start | bytes 3932160 | tf_op jit(solution)/shard_map/all_gather | solution.py:172
  208.0 2.2 slice-start
  209.6 110.6 %all-gather.14.cloned.1.call-start = ((), (), s32[]{:S(2)}) async-start(), calls=%async_computation.12 | async-start | bytes 3932160 | tf_op jit(solution)/shard_map/all_gather | solution.py:100
  210.2 185.3 %reduce-scatter.13.cloned.1.call-start = ((), (), s32[]{:S(2)}) async-start(), calls=%async_computation.13 | async-start | bytes 7864320 | tf_op jit(solution)/shard_map/reduce_scatter | solution.py:197
  320.2 12.3 %copy-start.32 = (bf16[2,768,768]{2,1,0:T(8,128)(2,1)S(1)}, bf16[2,768,768]{2,1,0:T(8,128)(2,1)}, u32[]{:S(2)}) copy-start(bf16[2,768,768]{2,1,0:T(8,128)(2,1)} %all-gather.12.cloned.1.call-done) | copy-start | bytes 7077892
  330.8 1.6 copy-start.33
  337.0 99.1 %reduce-scatter.11.cloned.1.call-start = ((), (), s32[]{:S(2)}) async-start(), calls=%async_computation.11 | async-start | bytes 3932160 | tf_op jit(solution)/shard_map/reduce_scatter | solution.py:178
  343.6 92.4 %copy-start.29 = (f32[768]{0:T(1024)S(1)}, f32[768]{0:T(1024)}, u32[]{:S(2)}) copy-start(f32[768]{0:T(1024)} %get-tuple-element.527) | copy-start | bytes 9220
  343.6 262.3 %reduce-scatter.17.cloned.1.call-start = ((), (), s32[]{:S(2)}) async-start(), calls=%async_computation.15 | async-start | bytes 2654208 | tf_op jit(solution)/shard_map/reduce_scatter | solution.py:307
  439.6 1.1 copy-start.1
  439.6 2.4 copy-start.8
  442.0 9.8 %collective-permute-start = (bf16[2,256,768]{2,1,0:T(8,128)(2,1)}, bf16[2,256,768]{2,1,0:T(8,128)(2,1)S(1)}, u32[]{:S(2)}, u32[]{:S(2)}) collective-permute-start(bf16[2,256,768]{2,1,0:T(8,128)(2,1)} %get-tuple-element.504), channel_id=1, source_target_pairs={{0,3},{1,0},{2,1},{3,2},{4,7},{5,4},{6,5},{7,6},{8,11},{9,8},{10,9... | collective-permute-start | bytes 2359304 | tf_op jit(solution)/shard_map/ppermute | solution.py:23
  442.0 13.7 %copy-start.31 = (bf16[2,1024,768]{2,1,0:T(8,128)(2,1)S(1)}, bf16[2,1024,768]{2,1,0:T(8,128)(2,1)}, u32[]{:S(2)}) copy-start(bf16[2,1024,768]{2,1,0:T(8,128)(2,1)} %all-gather.14.cloned.1.call-done) | copy-start | bytes 9437188
  454.2 6.4 copy-start.30
  454.2 6.4 copy-start.34
  454.2 37.0 %collective-permute-start.1 = (bf16[2,512,768]{2,1,0:T(8,128)(2,1)}, bf16[2,512,768]{2,1,0:T(8,128)(2,1)}, u32[]{:S(2)}, u32[]{:S(2)}) collective-permute-start(bf16[2,512,768]{2,1,0:T(8,128)(2,1)} %pad_maximum_fusion.1), channel_id=1, source_target_pairs={{0,2},{1,3},{2,0},{3,1},{4,6},{5,7},{6,4},{7,5},{8,10},{9,11},{10,... | collective-permute-start | bytes 4718600 | tf_op jit(solution)/shard_map/ppermute | solution.py:23
  465.0 196.7 %reduce-scatter.19.cloned.1.call-start = ((), (), s32[]{:S(2)}) async-start(), calls=%async_computation.16 | async-start | bytes 1327104
  501.7 1.7 copy-start.3
  504.6 2.8 copy-start.6
  519.1 1.8 copy-start.18
  522.1 1.7 copy-start.19
  535.2 1.8 copy-start.18
  538.2 1.6 copy-start.19
  551.3 1.8 copy-start.18
  554.2 1.6 copy-start.19
  567.4 1.8 copy-start.18
  570.3 1.6 copy-start.19
  582.0 2.6 copy-start.10
  584.3 2.7 copy-start.4
  584.5 3.6 copy-start.12
  584.5 5.5 copy-start.22
  596.1 105.3 %reduce-scatter.15.cloned.1.call-start = ((), (), s32[]{:S(2)}) async-start(), calls=%async_computation.14 | async-start | bytes 3932160 | tf_op jit(solution)/shard_map/reduce_scatter | solution.py:262
  602.4 1.0 copy-start.16
  602.4 1.2 copy-start.21
  602.4 3.5 copy-start.15
  609.2 92.2 %copy-start.26 = (f32[768]{0:T(1024)S(1)}, f32[768]{0:T(1024)}, u32[]{:S(2)}) copy-start(f32[768]{0:T(1024)} %copy-done.25) | copy-start | bytes 9220
  663.9 79.7 %copy-start.24 = (f32[12,768]{1,0:T(8,128)S(1)}, f32[12,768]{1,0:T(8,128)}, u32[]{:S(2)}) copy-start(f32[12,768]{1,0:T(8,128)} %param.25) | copy-start | bytes 110596
  663.9 79.7 %copy-start.27 = (f32[12,768]{1,0:T(8,128)S(1)}, f32[12,768]{1,0:T(8,128)}, u32[]{:S(2)}) copy-start(f32[12,768]{1,0:T(8,128)} %param.26) | copy-start | bytes 110596
  663.9 79.7 %copy-start.28 = (f32[12,768]{1,0:T(8,128)S(1)}, f32[12,768]{1,0:T(8,128)}, u32[]{:S(2)}) copy-start(f32[12,768]{1,0:T(8,128)} %param.27) | copy-start | bytes 110596
  665.1 79.3 %copy-start.2 = (f32[2,256,768]{2,1,0:T(8,128)S(1)}, f32[2,256,768]{2,1,0:T(8,128)}, u32[]{:S(2)}) copy-start(f32[2,256,768]{2,1,0:T(8,128)} %copy-done.1) | copy-start | bytes 4718596
  701.4 43.0 %copy-start.13 = (bf16[2,256,768]{2,1,0:T(8,128)(2,1)S(1)}, bf16[2,256,768]{2,1,0:T(8,128)(2,1)}, u32[]{:S(2)}) copy-start(bf16[2,256,768]{2,1,0:T(8,128)(2,1)} %reduce-scatter.15.cloned.1.call-done) | copy-start | bytes 2359300
  743.6 3.7 copy-start.23
Sparse Core Ops, SparseCore 0:
  10.8 46.8 all-gather.7
  59.2 27.3 all-gather.5
  147.8 58.3 reduce-scatter.8
  209.0 51.9 all-gather.11
  263.0 27.0 all-gather.9
  291.6 28.5 all-gather.13
  337.1 58.3 reduce-scatter.12
  398.0 37.9 reduce-scatter.10
  465.1 70.1 reduce-scatter.16
  596.2 65.4 reduce-scatter.18
  664.4 36.9 reduce-scatter.14
